TPU v7x, 256 devices: a whole 4x4x8 slice. The times are simulated.
256 devices in a mesh: wide: 64 (over x, z, core), narrow: 4 (over y).
Axes of the slice: x: 4, y: 4, z: 8, core: 2. Of those that a mesh axis runs over, the one named last changes fastest.
Arguments:
- dosage: bfloat16 [262144, 4096], P(('wide', 'narrow')), may hold values from 0 to 2
- keep_rows: int32 [229376], P(('wide', 'narrow')), may hold values from 0 to 1023, as said below
- allele_counts: int32 [4096], replicated, may hold values from 157286 to 367000, as said below
- projection: bfloat16 [4096, 128], replicated, may hold values from -0.09375 to 0.09375
Outputs:
- scores: float32 [229376, 128], P(('wide', 'narrow'))
- loadings: float32 [4096, 128], P('narrow')
Inputs may be any that keep to these rules, and one draw needn't show every extreme that they name: `keep_rows`: each block of 896 entries holds distinct local row numbers of one device's 1024 samples, ascending. `allele_counts`: totals over all 262144 genotyped samples, before outlier removal.
All inputs are finite; a program needn't handle non-finite values.
Results may differ from a plain program's by a relative error of at most 0.0075.
The roundings to bfloat16 on the way count: a program that leaves them out, or rounds other values in their place, can miss the bound.
Values sent between devices are 32-bit elements; how exact they have to be, the bound alone decides.
A program may use at most 64 MiB of HBM per device.

v0:
```python
import math
import jax
import jax.numpy as jnp
from jax import lax
from jax.sharding import PartitionSpec as P

ITERS = 2


def transposed_product(left_side, right_side):
    return lax.dot_general(
        left_side, right_side, (((0,), (0,)), ((), ())), preferred_element_type=jnp.float32
    )


def invert_factor(gram_matrix):
    lower_factor = jnp.linalg.cholesky(gram_matrix)
    unit_matrix = jnp.eye(gram_matrix.shape[0], dtype=jnp.float32)
    return jax.scipy.linalg.solve_triangular(lower_factor, unit_matrix, lower=True)


def on_device(dosage, keep_rows, allele_counts, projection):
    groups = lax.axis_size("wide") * lax.axis_size("narrow")
    samples_total = dosage.shape[0] * groups
    kept_total = keep_rows.shape[0] * groups
    snp_count = dosage.shape[1]
    narrow_size = lax.axis_size("narrow")
    share_rows = snp_count // narrow_size
    position = lax.axis_index("narrow")
    frequency = allele_counts.astype(jnp.float32) / (2.0 * samples_total)
    center = 2.0 * frequency
    spread = jnp.sqrt(2.0 * frequency * (1.0 - frequency))
    chosen = jnp.take(dosage, keep_rows, axis=0)
    standard = ((chosen.astype(jnp.float32) - center) / spread).astype(jnp.bfloat16)
    projected = jnp.dot(standard, projection, preferred_element_type=jnp.float32).astype(
        jnp.bfloat16
    )
    inverse = None
    loadings = None
    for iteration in range(ITERS):
        last_turn = iteration + 1 == ITERS
        gram_matrix = None
        gram_matrix = lax.psum(transposed_product(projected, projected), ("wide", "narrow"))
        totals = lax.psum(transposed_product(standard, projected), ("wide", "narrow"))
        inverse = invert_factor(gram_matrix)
        loadings_all = jnp.dot(totals, inverse.T, precision=lax.Precision.HIGHEST)
        if last_turn:
            loadings = lax.dynamic_slice_in_dim(loadings_all, position * share_rows, share_rows, 0)
        else:
            projected = jnp.dot(
                standard, loadings_all.astype(jnp.bfloat16), preferred_element_type=jnp.float32
            ).astype(jnp.bfloat16)
    scores = jnp.dot(
        projected.astype(jnp.float32), inverse.T, precision=lax.Precision.HIGHEST
    ) * math.sqrt(kept_total)
    return (scores, loadings)


def solution(mesh):
    in_specs = (P(("wide", "narrow"), None), P(("wide", "narrow")), P(), P())
    out_specs = (P(("wide", "narrow"), None), P("narrow", None))
    return jax.shard_map(
        on_device, mesh=mesh, in_specs=in_specs, out_specs=out_specs, check_vma=False
    )
```

profile of v0, /device:TPU:8, one launch (start us, length us, event | category | flops | bytes accessed | tf_op | source)
XLA Modules:
  0.0 645.3 jit_solution(8097715273102711557)
XLA Ops:
  7.2 0.8 compare_select_fusion
  8.7 0.7 convert_multiply_fusion
  9.4 19.5 %gather_fusion = bf16[896,4096]{1,0:T(8,128)(2,1)} fusion(bf16[1024,4096]{1,0:T(8,128)(2,1)} %param.7, s32[1024]{0:T(1024)S(1)} %pad_clamp_fusion), kind=kCustom, calls=%fused_computation | custom fusion | bytes 14683648 | tf_op jit(solution)/shard_map/jit(_take)/gather | solution.py:33
  28.9 6.6 %divide_convert_fusion = bf16[896,4096]{1,0:T(8,128)(2,1)S(1)} fusion(f32[4096]{0:T(1024)S(1)} %get-tuple-element.9, f32[4096]{0:T(1024)S(1)} %get-tuple-element.8, bf16[896,4096]{1,0:T(8,128)(2,1)} %gather_fusion, pred[896]{0:T(1024)(128)(4,1)S(1)} %compare_and_fusion), kind=kLoop, calls=%fused_computation.1 | loop fusion | flops 18350080 | bytes 14713728 | tf_op jit(solution)/shard_map/convert_element_type | solution.py:34
  35.5 2.1 convolution_convert_fusion.2
  37.6 3.5 fusion.10
  41.1 0.9 fusion.11
  42.3 266.6 %all-reduce.7.cloned.1.call-done = (f32[4096,128]{1,0:T(8,128)}, f32[128,128]{0,1:T(8,128)}) async-done(((f32[4096,128]{1,0:T(8,128)}, f32[128,128]{0,1:T(8,128)}), (f32[4096,128]{1,0:T(8,128)}, f32[128,128]{0,1:T(8,128)})) %all-reduce.7.cloned.1.call-update) | async-done | bytes 2162704 | tf_op jit(solution)/shard_map/psum | solution.py:44
  308.9 0.9 copy.7
  309.8 0.9 fusion.9
  310.6 11.7 %cholesky.44 = f32[128,128]{1,0:T(8,128)S(1)} custom-call(f32[128,128]{1,0:T(8,128)S(1)} %fusion.9), custom_call_target="Cholesky" | custom-call | tf_op jit(solution)/shard_map/jit(cholesky)/cholesky | solution.py:17
  323.7 9.8 %custom-call.6 = f32[1,128,128]{1,2,0:T(8,128)S(1)} custom-call(f32[1,128,128]{2,1,0:T(8,128)S(1)} %fusion.4), custom_call_target="InvertDiagBlocksLowerTriangular" | custom-call | tf_op jit(solution)/shard_map/jit(_solve_triangular)/triangular_solve | solution.py:19
  333.8 3.5 convolution_convert_fusion
  337.4 5.3 convolution_convert_fusion.1
  342.7 3.5 fusion.13
  346.2 0.9 fusion.12
  347.1 260.8 %all-reduce.5.cloned.1.call-done = (f32[128,128]{0,1:T(8,128)}, f32[4096,128]{1,0:T(8,128)}) async-done(((f32[128,128]{0,1:T(8,128)}, f32[4096,128]{1,0:T(8,128)}), (f32[128,128]{0,1:T(8,128)}, f32[4096,128]{1,0:T(8,128)})) %all-reduce.5.cloned.1.call-update) | async-done | bytes 2162704 | tf_op jit(solution)/shard_map/psum | solution.py:43
  607.9 1.1 copy.9
  609.0 0.9 fusion.7
  609.9 11.7 %cholesky.55 = f32[128,128]{1,0:T(8,128)S(1)} custom-call(f32[128,128]{1,0:T(8,128)S(1)} %fusion.7), custom_call_target="Cholesky" | custom-call | tf_op jit(solution)/shard_map/jit(cholesky)/cholesky | solution.py:17
  623.0 9.8 %custom-call.7 = f32[1,128,128]{1,2,0:T(8,128)S(1)} custom-call(f32[1,128,128]{2,1,0:T(8,128)S(1)} %fusion.5), custom_call_target="InvertDiagBlocksLowerTriangular" | custom-call | tf_op jit(solution)/shard_map/jit(_solve_triangular)/triangular_solve | solution.py:19
  633.1 1.1 convolution_multiply_fusion
  634.2 3.5 fusion.14
  637.7 0.8 constant_dynamic-slice_fusion
  (23 shorter events, 4.3 us)
Async XLA Ops:
  7.2 28.3 %copy-start = (bf16[4096,128]{1,0:T(8,128)(2,1)S(1)}, bf16[4096,128]{1,0:T(8,128)(2,1)}, u32[]{:S(2)}) copy-start(bf16[4096,128]{1,0:T(8,128)(2,1)} %param.10) | copy-start | bytes 3145732
  7.2 301.7 %all-reduce.7.cloned.1.call-start = ((), (), s32[]{:S(2)}) async-start(), calls=%async_computation.1 | async-start | bytes 4325376 | tf_op jit(solution)/shard_map/psum | solution.py:44
  35.5 5.6 copy-start.1
  42.0 565.9 %all-reduce.5.cloned.1.call-start = ((), (), s32[]{:S(2)}) async-start(), calls=%async_computation | async-start | bytes 4325376 | tf_op jit(solution)/shard_map/psum | solution.py:43
  333.8 8.9 %slice-start = ((s8[7340032]{0:T(1024)(128)(4,1)}), s8[4194304]{0:T(1024)(128)(4,1)S(1)}, s32[]{:S(2)}) async-start(s8[7340032]{0:T(1024)(128)(4,1)} %bitcast.36), calls=%async_computation.2 | async-start | bytes 8388608
  337.4 5.3 slice-start.1
Sparse Core Ops, SparseCore 0:
  42.2 266.6 all-reduce.6
  347.3 260.5 all-reduce.4
where the time goes:
time: 646 us; the launch traced here: 645 us
  waiting for transfers between devices  527 us (82%)
  other arithmetic  56.2 us (9%)
  matrix products  24.9 us (4%)
  local copies, waits for them, and re-layouts  22.4 us (3%)
  between operations  14.2 us (2%)
    psum x1, waiting for transfers between devices, on_device(): lax.psum(transposed_product(standard, projected), ('wide', 'narrow'))  267 us
    psum x1, waiting for transfers between devices, on_device(): lax.psum(transposed_product(projected, projected), ('wide', 'narrow'))  261 us
    another operation x6, other arithmetic, invert_factor(): lower_factor = jnp.linalg.cholesky(gram_matrix)  24.8 us
    another operation x4, other arithmetic, invert_factor(): jax.scipy.linalg.solve_triangular(lower_factor, unit_matrix, lower=True)  20.9 us
    gather x1, local copies, waits for them, and re-layouts, on_device(): chosen = jnp.take(dosage, keep_rows, axis=0)  19.5 us
  transfers between devices with their start and end apart: 2, of which 2 were waited for; matrix products, arithmetic and copies ran while one was open for 0% of the time, Pallas kernels for 0%

commit v1 on v0

--- a/solution.py
+++ b/solution.py
@@ -40,7 +40,9 @@
     for iteration in range(ITERS):
         last_turn = iteration + 1 == ITERS
         gram_matrix = None
-        gram_matrix = lax.psum(transposed_product(projected, projected), ("wide", "narrow"))
+        gram_matrix = jnp.sum(
+            lax.all_gather(transposed_product(projected, projected), ("wide", "narrow")), axis=0
+        )
         totals = lax.psum(transposed_product(standard, projected), ("wide", "narrow"))
         inverse = invert_factor(gram_matrix)
         loadings_all = jnp.dot(totals, inverse.T, precision=lax.Precision.HIGHEST)

time: 646 us -> 847 us (1.31)
  waiting for transfers between devices: 527 us -> 710 us
  other arithmetic: 56.2 us -> 67.8 us
    psum x1 -> x0, waiting for transfers between devices: 261 us -> none  [on_device(): lax.psum(transposed_product(projected, projected), ('wide', 'narrow'))]
    all_gather x0 -> x2, waiting for transfers between devices: none -> 239 us  [on_device(): lax.all_gather(transposed_product(projected, projected), ('wide', 'narrow'))]
    psum x1 -> x2, waiting for transfers between devices: 267 us -> 472 us  [on_device(): lax.psum(transposed_product(standard, projected), ('wide', 'narrow'))]
    reduce_sum x0 -> x2, other arithmetic: none -> 13.3 us  [on_device(): jnp.sum(lax.all_gather(transposed_product(projected, projected), ('wide',...]
  transfers between devices with their start and end apart: 2 -> 4, of which waited for: 2 -> 4; matrix products, arithmetic and copies ran while one was open for 0% -> 9% of each run, Pallas kernels for 0% -> 0%
where the time goes in v1:
time: 847 us
  waiting for transfers between devices  710 us (84%)
  other arithmetic  67.8 us (8%)
  matrix products  30.6 us (4%)
  local copies, waits for them, and re-layouts  23.5 us (3%)
  between operations  13.9 us (2%)
    psum x2, waiting for transfers between devices, on_device(): lax.psum(transposed_product(standard, projected), ('wide', 'narrow'))  472 us
    all_gather x2, waiting for transfers between devices, on_device(): lax.all_gather(transposed_product(projected, projected), ('wide', 'narrow'))  239 us
    another operation x6, other arithmetic, invert_factor(): lower_factor = jnp.linalg.cholesky(gram_matrix)  24.8 us
    another operation x4, other arithmetic, invert_factor(): jax.scipy.linalg.solve_triangular(lower_factor, unit_matrix, lower=True)  20.9 us
    gather x1, local copies, waits for them, and re-layouts, on_device(): chosen = jnp.take(dosage, keep_rows, axis=0)  19.5 us
  transfers between devices with their start and end apart: 4, of which 4 were waited for; matrix products, arithmetic and copies ran while one was open for 9% of the time, Pallas kernels for 0%

profile of v1, /device:TPU:8, one launch (start us, length us, event | category | flops | bytes accessed | tf_op | source)
XLA Modules:
  0.0 846.7 jit_solution(17544723986587139861)
XLA Ops:
  7.2 0.8 compare_select_fusion
  9.4 19.5 %gather_fusion = bf16[896,4096]{1,0:T(8,128)(2,1)} fusion(bf16[1024,4096]{1,0:T(8,128)(2,1)} %param.7, s32[1024]{0:T(1024)S(1)} %pad_clamp_fusion), kind=kCustom, calls=%fused_computation | custom fusion | bytes 14683648 | tf_op jit(solution)/shard_map/jit(_take)/gather | solution.py:33
  28.9 6.6 divide_convert_fusion
  35.5 3.0 copy-done.2
  38.5 2.1 convolution_convert_fusion.2
  40.5 0.9 fusion.11
  41.5 6.5 fusion.10
  48.2 121.4 %all-gather.5.cloned.1.call-done = f32[32768,128]{1,0:T(8,128)} async-done(((f32[128,128]{1,0:T(8,128)}), f32[32768,128]{1,0:T(8,128)}) %all-gather.5.cloned.1.call-update) | async-done | bytes 16777232 | tf_op jit(solution)/shard_map/all_gather | solution.py:44
  169.7 6.6 reduce_sum.18
  176.4 11.7 %cholesky.44 = f32[128,128]{1,0:T(8,128)S(1)} custom-call(f32[128,128]{1,0:T(8,128)S(1)} %fusion.9), custom_call_target="Cholesky" | custom-call | tf_op jit(solution)/shard_map/jit(cholesky)/cholesky | solution.py:17
  189.4 9.8 %custom-call.6 = f32[1,128,128]{1,2,0:T(8,128)S(1)} custom-call(f32[1,128,128]{2,1,0:T(8,128)S(1)} %fusion.4), custom_call_target="InvertDiagBlocksLowerTriangular" | custom-call | tf_op jit(solution)/shard_map/jit(_solve_triangular)/triangular_solve | solution.py:19
  199.5 236.5 %all-reduce.3.cloned.1.call-done = f32[4096,128]{1,0:T(8,128)} async-done(((f32[4096,128]{1,0:T(8,128)}), f32[4096,128]{1,0:T(8,128)}) %all-reduce.3.cloned.1.call-update) | async-done | bytes 2097168 | tf_op jit(solution)/shard_map/psum | solution.py:46
  436.0 3.4 convolution_convert_fusion
  439.4 5.1 convolution_convert_fusion.1
  444.6 0.9 fusion.12
  445.7 6.6 fusion.13
  452.3 117.4 %all-gather.7.cloned.1.call-done = f32[32768,128]{1,0:T(8,128)} async-done(((f32[128,128]{1,0:T(8,128)}), f32[32768,128]{1,0:T(8,128)}) %all-gather.7.cloned.1.call-update) | async-done | bytes 16777232 | tf_op jit(solution)/shard_map/all_gather | solution.py:44
  569.7 6.7 reduce_sum.19
  576.5 11.7 %cholesky.55 = f32[128,128]{1,0:T(8,128)S(1)} custom-call(f32[128,128]{1,0:T(8,128)S(1)} %fusion.7), custom_call_target="Cholesky" | custom-call | tf_op jit(solution)/shard_map/jit(cholesky)/cholesky | solution.py:17
  589.6 9.8 %custom-call.7 = f32[1,128,128]{1,2,0:T(8,128)S(1)} custom-call(f32[1,128,128]{2,1,0:T(8,128)S(1)} %fusion.5), custom_call_target="InvertDiagBlocksLowerTriangular" | custom-call | tf_op jit(solution)/shard_map/jit(_solve_triangular)/triangular_solve | solution.py:19
  599.7 1.1 convolution_multiply_fusion
  600.8 235.0 %all-reduce.5.cloned.1.call-done = f32[4096,128]{1,0:T(8,128)} async-done(((f32[4096,128]{1,0:T(8,128)}), f32[4096,128]{1,0:T(8,128)}) %all-reduce.5.cloned.1.call-update) | async-done | bytes 2097168 | tf_op jit(solution)/shard_map/psum | solution.py:46
  835.8 3.5 fusion.14
  839.3 0.8 constant_dynamic-slice_fusion
  (28 shorter events, 5.5 us)
Async XLA Ops:
  7.2 31.3 %copy-start = (bf16[4096,128]{1,0:T(8,128)(2,1)S(1)}, bf16[4096,128]{1,0:T(8,128)(2,1)}, u32[]{:S(2)}) copy-start(bf16[4096,128]{1,0:T(8,128)(2,1)} %param.10) | copy-start | bytes 3145732
  7.2 162.5 %all-gather.5.cloned.1.call-start = ((), (), s32[]{:S(2)}) async-start(), calls=%async_computation.2 | async-start | bytes 16842752 | tf_op jit(solution)/shard_map/all_gather | solution.py:44
  35.5 3.0 copy-start.2
  41.4 394.6 %all-reduce.3.cloned.1.call-start = ((), (), s32[]{:S(2)}) async-start(), calls=%async_computation | async-start | bytes 4194304 | tf_op jit(solution)/shard_map/psum | solution.py:46
  48.0 521.7 %all-gather.7.cloned.1.call-start = ((), (), s32[]{:S(2)}) async-start(), calls=%async_computation.3 | async-start | bytes 16842752 | tf_op jit(solution)/shard_map/all_gather | solution.py:44
  445.5 390.4 %all-reduce.5.cloned.1.call-start = ((), (), s32[]{:S(2)}) async-start(), calls=%async_computation.1 | async-start | bytes 4194304 | tf_op jit(solution)/shard_map/psum | solution.py:46
  569.7 270.4 %copy-start.1 = (bf16[4096,128]{1,0:T(8,128)(2,1)S(1)}, bf16[4096,128]{1,0:T(8,128)(2,1)}, u32[]{:S(2)}) copy-start(bf16[4096,128]{1,0:T(8,128)(2,1)} %param.10) | copy-start | bytes 3145732
Sparse Core Ops, SparseCore 0:
  41.6 128.0 all-gather.4
  175.0 260.9 all-reduce.2
  445.6 124.0 all-gather.6
  574.9 260.8 all-reduce.4
